TPU v7x, 32 devices: a whole 2x2x4 slice. The times are simulated.
32 devices in a mesh: groups: 2 (over y), seq: 8 (over z, x), chan: 1, section: 2 (over core).
Axes of the slice: x: 2, y: 2, z: 4, core: 2. Of those that a mesh axis runs over, the one named last changes fastest.
Arguments:
- queries: bfloat16 [8192, 8192], P(('groups', 'seq', 'section'), 'chan'), parts along dimension 0, may hold values from -6 to 6
- key_proj: bfloat16 [8192, 8192], P(('groups', 'seq', 'section'), 'chan'), parts along dimension 0, may hold values from -6 to 6
- value_proj: bfloat16 [8192, 8192], P(('groups', 'seq', 'section'), 'chan'), parts along dimension 0, may hold values from -6 to 6
- filter_taps: bfloat16 [512, 128], P('chan'), may hold values from -0.5 to 0.5
- skip_gain: float32 [8192], P('chan'), may hold values from -3 to 3
- out_weight: bfloat16 [8192, 4096], P('chan', ('seq', 'section')), may hold values from -0.09375 to 0.09375
- residual: bfloat16 [8192, 4096], P(('groups', 'seq', 'section'), 'chan'), parts along dimension 0, may hold values from -6 to 6
Outputs:
- layer_out: bfloat16 [8192, 4096], P(('groups', 'seq', 'section'), 'chan'), parts along dimension 0
There are 2 independent parts, one for each index of `groups`. A program takes and returns all parts, laid end to end along the dimension named above; an argument that names none is the same for every part. Nothing has to cross between parts.
All inputs are finite; a program needn't handle non-finite values.
Results may differ from a plain program's by a relative error of at most 0.0053.
Values may be sent and summed in bfloat16 or wider, within the bound.
A program may use at most 256 MiB of HBM per device.

v0:
```python
import jax
import jax.numpy as jnp
from jax import lax
from jax.sharding import PartitionSpec as P


def shifted(value, axis, steps):
    count = lax.axis_size(axis)
    initial, last = (max(0, -steps), min(count, count - steps))
    return lax.ppermute(value, axis, [(source, source + steps) for source in range(initial, last)])


def filter_matrices(filter_taps):
    groups_here, block_len = filter_taps.shape
    pattern = jnp.concatenate(
        [
            jnp.zeros((groups_here, 1), filter_taps.dtype),
            filter_taps[:, ::-1],
            jnp.zeros((groups_here, block_len), filter_taps.dtype),
        ],
        axis=1,
    )
    tiled = jnp.tile(pattern, (1, block_len))[:, : block_len * 2 * block_len]
    both = tiled.reshape(groups_here, block_len, 2 * block_len)
    return (both[:, :, block_len:], both[:, :, :block_len])


def apply_blocks(matrix, blocks):
    return jnp.einsum("gij,bjgc->bigc", matrix, blocks, preferred_element_type=jnp.float32)


def body(queries, key_proj, value_proj, filter_taps, skip_gain, out_weight, residual):
    seq_len, channels = queries.shape
    groups_here, block_len = filter_taps.shape
    per_group = channels // groups_here
    block_count = seq_len // block_len
    product = (key_proj.astype(jnp.float32) * value_proj.astype(jnp.float32)).astype(jnp.bfloat16)
    blocks = product.reshape(block_count, block_len, groups_here, per_group)
    now_matrix, prev_matrix = filter_matrices(filter_taps)
    convolved = apply_blocks(now_matrix, blocks)
    carried = apply_blocks(prev_matrix, blocks)
    outgoing = carried[block_count - 1, : block_len - 1].reshape(block_len - 1, channels)
    incoming = shifted(outgoing, ("seq", "section"), 1)
    first = jnp.concatenate([incoming, jnp.zeros((1, channels), jnp.float32)], axis=0)
    first = first.reshape(1, block_len, groups_here, per_group)
    carried = jnp.concatenate([first, carried[: block_count - 1]], axis=0)
    convolved = (convolved + carried).reshape(seq_len, channels)
    gated = (
        queries.astype(jnp.float32) * (convolved + skip_gain[None, :] * product.astype(jnp.float32))
    ).astype(jnp.bfloat16)
    partial_out = jnp.dot(
        gated,
        lax.all_gather(out_weight, ("seq", "section"), axis=1, tiled=True),
        preferred_element_type=jnp.float32,
    )
    out_share = lax.psum_scatter(partial_out, "chan", scatter_dimension=1, tiled=True)
    return (residual.astype(jnp.float32) + out_share).astype(jnp.bfloat16)


def solution(mesh):
    return jax.shard_map(
        body,
        mesh=mesh,
        in_specs=(
            P(("groups", "seq", "section"), "chan"),
            P(("groups", "seq", "section"), "chan"),
            P(("groups", "seq", "section"), "chan"),
            P("chan", None),
            P("chan"),
            P("chan", ("seq", "section")),
            P(("groups", "seq", "section"), "chan"),
        ),
        out_specs=P(("groups", "seq", "section"), "chan"),
        check_vma=False,
    )
```

profile of v0, /device:TPU:0, one launch (start us, length us, event | category | flops | bytes accessed | tf_op | source)
XLA Modules:
  0.0 429.6 jit_solution(3508828686068066326)
XLA Ops:
  6.5 0.7 all-gather.2.cloned.1.call-update
  7.3 6.4 %copy.11 = bf16[256,8192]{0,1:T(8,128)(2,1)} copy(bf16[256,8192]{1,0:T(8,128)(2,1)} %param.8) | data formatting | bytes 8388608 | tf_op args[1]
  13.6 6.6 %copy.12 = bf16[256,8192]{0,1:T(8,128)(2,1)} copy(bf16[256,8192]{1,0:T(8,128)(2,1)} %param.9) | data formatting | bytes 8388608 | tf_op args[2]
  20.2 6.8 %multiply_convert_fusion = bf16[256,8192]{0,1:T(8,128)(2,1)} fusion(bf16[256,8192]{0,1:T(8,128)(2,1)} %copy.12, bf16[256,8192]{0,1:T(8,128)(2,1)} %copy.11), kind=kLoop, calls=%fused_computation.8 | loop fusion | flops 8388608 | bytes 12582912 | tf_op jit(solution)/shard_map/convert_element_type | solution.py:37
  27.0 7.0 %reshape.17 = bf16[2,128,512,16]{1,0,3,2:T(2,128)(2,1)} reshape(bf16[256,8192]{0,1:T(8,128)(2,1)} %multiply_convert_fusion) | data formatting | bytes 8388608 | tf_op jit(solution)/shard_map/reshape | solution.py:38
  34.0 0.4 rev.3
  34.4 0.1 maximum_maximum_fusion
  34.6 0.2 copy.13
  34.8 11.6 %tile.4 = bf16[512,128,257]{0,2,1:T(8,128)(2,1)} broadcast(bf16[512,257]{0,1:T(8,128)(2,1)S(1)} %copy.13), dimensions={0,2} | broadcast | bytes 33948672 | tf_op jit(solution)/shard_map/tile | solution.py:23
  46.4 30.7 %tile.10 = bf16[512,32896]{0,1:T(8,128)(2,1)} reshape(bf16[512,128,257]{0,2,1:T(8,128)(2,1)} %tile.4) | data formatting | bytes 67371008 | tf_op jit(solution)/shard_map/tile | solution.py:23
  77.0 23.3 %slice.20 = bf16[512,32768]{0,1:T(8,128)(2,1)} slice(bf16[512,32896]{0,1:T(8,128)(2,1)} %tile.10), slice={[0:512], [0:32768]} | slice | bytes 67108864 | tf_op jit(solution)/shard_map/slice | solution.py:23
  100.4 24.4 %fusion.20 = (bf16[512,128,128]{0,2,1:T(8,128)(2,1)}, bf16[512,128,128]{0,2,1:T(8,128)(2,1)}) fusion(bf16[512,128,256]{0,2,1:T(8,128)(2,1)} %bitcast.38), kind=kLoop, calls=%fused_computation.16 | loop fusion | bytes 67108864 | tf_op jit(solution)/shard_map/slice | solution.py:25
  124.8 23.7 %copy.22 = bf16[512,128,128]{2,1,0:T(8,128)(2,1)} copy(bf16[512,128,128]{0,2,1:T(8,128)(2,1)} %get-tuple-element.6) | data formatting | bytes 33554432
  148.5 15.3 %fusion.11 = f32[2,128,512,16]{1,3,0,2:T(8,128)} fusion(bf16[512,128,128]{2,1,0:T(8,128)(2,1)} %copy.22, bf16[2,128,512,16]{1,0,3,2:T(2,128)(2,1)} %reshape.17), kind=kOutput, calls=%fused_computation.14 | convolution fusion | flops 536870912 | bytes 29360128 | tf_op jit(solution)/shard_map/gij,bjgc->bigc/dot_general | solution.py:29
  163.8 4.9 %slice.23 = f32[1,127,512,16]{1,3,0,2:T(8,128)} slice(f32[2,128,512,16]{1,3,0,2:T(8,128)} %fusion.11), slice={[1:2], [0:127], [0:512], [0:16]} | slice | bytes 8323072 | tf_op jit(solution)/shard_map/slice | solution.py:42
  168.7 4.8 %collective-permute-start = (f32[127,8192]{0,1:T(8,128)}, f32[127,8192]{0,1:T(8,128)}, u32[]{:S(2)}, u32[]{:S(2)}) collective-permute-start(f32[127,8192]{0,1:T(8,128)} %bitcast.7), channel_id=1, source_target_pairs={{0,1},{1,2},{2,3},{3,4},{4,5},{5,6},{6,7},{7,8},{8,9},{9,10},{10,1... | collective-permute-start | bytes 12484616 | tf_op jit(solution)/shard_map/ppermute | solution.py:10
  173.5 2.5 slice.24
  175.9 23.7 %copy.21 = bf16[512,128,128]{2,1,0:T(8,128)(2,1)} copy(bf16[512,128,128]{0,2,1:T(8,128)(2,1)} %get-tuple-element.5) | data formatting | bytes 33554432
  199.6 6.4 %copy.10 = bf16[256,8192]{0,1:T(8,128)(2,1)} copy(bf16[256,8192]{1,0:T(8,128)(2,1)} %param.7) | data formatting | bytes 8388608 | tf_op args[0]
  206.0 5.0 %concatenate.10 = f32[128,8192]{0,1:T(8,128)} pad(f32[127,8192]{0,1:T(8,128)} %collective-permute-done, f32[]{:T(128)} %constant.0.clone.1), padding=0_1x0_0 | pad | bytes 8355844 | tf_op jit(solution)/shard_map/concatenate | solution.py:44
  211.1 16.4 %maximum_add_fusion = f32[2,128,512,16]{1,3,0,2:T(8,128)} fusion(f32[1,128,512,16]{1,3,0,2:T(8,128)} %slice.24, f32[1,128,512,16]{1,3,0,2:T(8,128)} %bitcast.40, bf16[512,128,128]{2,1,0:T(8,128)(2,1)} %copy.21, bf16[2,128,512,16]{1,0,3,2:T(2,128)(2,1)} %reshape.17), kind=kOutput, calls=%fused_computation.7 | convolution fusion | flops 541065216 | bytes 37748736 | tf_op jit(solution)/shard_map/gij,bjgc->bigc/dot_general | solution.py:29
  227.5 13.4 %copy.17 = f32[2,128,512,16]{1,0,3,2:T(2,128)} copy(f32[2,128,512,16]{1,3,0,2:T(8,128)} %maximum_add_fusion) | data formatting | bytes 16777216 | tf_op jit(solution)/shard_map/add | solution.py:47
  240.9 150.1 %all-gather.2.cloned.1.call-done = bf16[8192,4096]{1,0:T(8,128)(2,1)} async-done(((bf16[8192,256]{1,0:T(8,128)(2,1)}), bf16[8192,4096]{1,0:T(8,128)(2,1)}) %all-gather.2.cloned.1.call-update) | async-done | bytes 67108880 | tf_op jit(solution)/shard_map/all_gather | solution.py:53
  390.9 31.8 %fusion.6 = bf16[256,4096]{1,0:T(8,128)(2,1)} fusion(bf16[8192,4096]{1,0:T(8,128)(2,1)} %all-gather.2.cloned.1.call-done, f32[1024,8,2,128]{3,2,1,0:T(2,128)} %bitcast.39, bf16[256,8192]{0,1:T(8,128)(2,1)} %multiply_convert_fusion, bf16[256,8192]{0,1:T(8,128)(2,1)} %copy.10, f32[8192]{0:T(1024)S(1)} %copy-done.3, bf16[256,4096]{1,0:T(8,128)(2,1)S(1)} %copy-done.1), kind=kOutput, calls=%fused_computation.10 | convolution fusion | flops 17195597824 | bytes 88113152 | tf_op jit(solution)/shard_map/dot_general | solution.py:51
  (13 shorter events, 0.1 us)
Async XLA Ops:
  6.5 384.4 %all-gather.2.cloned.1.call-start = ((), (), s32[]{:S(2)}) async-start(), calls=%async_computation | async-start | bytes 71303168 | tf_op jit(solution)/shard_map/all_gather | solution.py:53
  20.2 13.8 %copy-start.2 = (bf16[512,128]{1,0:T(8,128)(2,1)S(1)}, bf16[512,128]{1,0:T(8,128)(2,1)}, u32[]{:S(2)}) copy-start(bf16[512,128]{1,0:T(8,128)(2,1)} %param.10) | copy-start | bytes 393220
  163.8 9.7 %copy-start = (f32[2,128,512,16]{1,3,0,2:T(8,128)S(1)}, f32[2,128,512,16]{1,3,0,2:T(8,128)}, u32[]{:S(2)}) copy-start(f32[2,128,512,16]{1,3,0,2:T(8,128)} %fusion.11) | copy-start | bytes 25165828
  168.7 37.4 %collective-permute-start = (f32[127,8192]{0,1:T(8,128)}, f32[127,8192]{0,1:T(8,128)}, u32[]{:S(2)}, u32[]{:S(2)}) collective-permute-start(f32[127,8192]{0,1:T(8,128)} %bitcast.7), channel_id=1, source_target_pairs={{0,1},{1,2},{2,3},{3,4},{4,5},{5,6},{6,7},{7,8},{8,9},{9,10},{10,1... | collective-permute-start | bytes 12484616 | tf_op jit(solution)/shard_map/ppermute | solution.py:10
  227.5 163.4 %copy-start.1 = (bf16[256,4096]{1,0:T(8,128)(2,1)S(1)}, bf16[256,4096]{1,0:T(8,128)(2,1)}, u32[]{:S(2)}) copy-start(bf16[256,4096]{1,0:T(8,128)(2,1)} %param.13) | copy-start | bytes 6291460
  227.5 163.4 %copy-start.3 = (f32[8192]{0:T(1024)S(1)}, f32[8192]{0:T(1024)}, u32[]{:S(2)}) copy-start(f32[8192]{0:T(1024)} %param.11) | copy-start | bytes 98308
Sparse Core Ops, SparseCore 0:
  8.9 382.0 all-gather.1
where the time goes:
time: 432 us; the launch traced here: 430 us
  local copies, waits for them, and re-layouts  190 us (44%)
  waiting for transfers between devices  151 us (35%)
  matrix products  63.5 us (15%)
  between operations  13.4 us (3%)
  other arithmetic  6.9 us (2%)
  starting transfers between devices  4.79 us (1%)
    all_gather x1, waiting for transfers between devices, body(): lax.all_gather(out_weight, ('seq', 'section'), axis=1, tiled=True)  150 us
    unnamed x13, local copies, waits for them, and re-layouts  66.8 us
    another operation x2, local copies, waits for them, and re-layouts, filter_matrices(): tiled = jnp.tile(pattern, (1, block_len))[:, :block_len * 2 * block_len]  42.3 us
    dot_general x1, matrix products, body(): jnp.dot(gated, lax.all_gather(out_weight, ('seq', 'section'), axis=1, til...  31.8 us
    dot_general x2, matrix products, apply_blocks(): jnp.einsum('gij,bjgc->bigc', matrix, blocks, preferred_element_type=jnp.f...  31.7 us
    slice x1, local copies, waits for them, and re-layouts, filter_matrices(): return (both[:, :, block_len:], both[:, :, :block_len])  24.4 us
    slice x1, local copies, waits for them, and re-layouts, filter_matrices(): tiled = jnp.tile(pattern, (1, block_len))[:, :block_len * 2 * block_len]  23.3 us
    add x1, local copies, waits for them, and re-layouts, body(): convolved = (convolved + carried).reshape(seq_len, channels)  13.4 us
  transfers between devices with their start and end apart: 2, of which 1 were waited for; matrix products, arithmetic and copies ran while one was open for 53% of the time, Pallas kernels for 0%

commit v1 on v0

--- a/solution.py
+++ b/solution.py
@@ -1,6 +1,10 @@
+import functools
+
 import jax
 import jax.numpy as jnp
 from jax import lax
+from jax.experimental import pallas as pl
+from jax.experimental.pallas import tpu as pltpu
 from jax.sharding import PartitionSpec as P
 
 
@@ -57,9 +61,219 @@
     return (residual.astype(jnp.float32) + out_share).astype(jnp.bfloat16)
 
 
+LANES = 128
+PIECES = 4
+
+
+def mixer_kernel(
+    seq_count, per_group,
+    q_hbm, k_hbm, v_hbm, pattern_ref, skip_ref, w_hbm,
+    g_full, w_full,
+    q_buf, k_buf, v_buf, gated, tail, halo,
+    load_sem, local_sem, halo_sem, zsend, zrecv, ysend, yrecv, xsend, xrecv, csend, crecv, fsend, frecv,
+):
+    group, seq, chan, core = (lax.axis_index(a) for a in ("groups", "seq", "chan", "section"))
+    far, near = seq // 2, seq % 2
+    line = seq_count // 2
+    rows, channels = q_hbm.shape
+    depth, width = w_hbm.shape
+    block = tail.shape[0]
+    half = depth // 2
+    piece = half // PIECES
+    chunk = channels // PIECES
+    me = near * 2 + core
+
+    def place(s, c, g=group):
+        return (g, s, chan, c)
+
+    core_mate = place(seq, 1 - core)
+    near_mate = place(far * 2 + 1 - near, core)
+    group_mate = place(seq, core, 1 - group)
+    linear = seq * 2 + core
+    after = lax.rem(linear + 1, seq_count * 2)
+    before = lax.rem(linear + seq_count * 2 - 1, seq_count * 2)
+    after, before = place(after // 2, after % 2), place(before // 2, before % 2)
+
+    loads = [
+        pltpu.make_async_copy(src, dst, load_sem.at[i])
+        for i, (src, dst) in enumerate(((k_hbm, k_buf), (v_hbm, v_buf), (q_hbm, q_buf)))
+    ]
+    for load in loads:
+        load.start()
+    own_cols = pl.ds(pl.multiple_of(far * width, width), width)
+    keep = pltpu.make_async_copy(w_hbm, w_full.at[:, own_cols], local_sem.at[0])
+    keep.start()
+
+    barrier = pltpu.get_barrier_semaphore()
+    peers = [place(lax.rem(far + d, line) * 2 + near, core) for d in range(1, line)]
+    for peer in peers + [core_mate, near_mate, group_mate, after, before]:
+        pl.semaphore_signal(barrier, inc=1, device_id=peer, device_id_type=pl.DeviceIdType.MESH)
+    pl.semaphore_wait(barrier, len(peers) + 5)
+
+    def remote(src, dst, send, recv, device):
+        return pltpu.make_async_remote_copy(
+            src_ref=src, dst_ref=dst, send_sem=send, recv_sem=recv,
+            device_id=device, device_id_type=pl.DeviceIdType.MESH,
+        )
+
+    def span(which, p):
+        return pl.ds(pl.multiple_of(which * half + p * piece, piece), piece)
+
+    def cols(z):
+        return pl.ds(pl.multiple_of(z * width, width), width)
+
+    loads[0].wait()
+    loads[1].wait()
+    tail[...] = (
+        k_buf[rows - block :, :].astype(jnp.float32) * v_buf[rows - block :, :].astype(jnp.float32)
+    ).astype(jnp.bfloat16)
+    edge = remote(tail, halo, halo_sem.at[0], halo_sem.at[1], after)
+    edge.start()
+
+    def along(d, p):
+        return remote(
+            w_hbm.at[span(group, p), :], w_full.at[span(group, p), cols(far)],
+            zsend.at[d - 1, p], zrecv.at[d - 1, p], peers[d - 1],
+        )
+
+    def across(d, p, which):
+        part = w_full.at[span(which, p), cols(lax.rem(far + line - d, line))]
+        return remote(part, part, ysend.at[d - 1, p], yrecv.at[d - 1, p], group_mate)
+
+    for p in range(PIECES):
+        for d in range(1, line):
+            along(d, p).start()
+
+    loads[2].wait()
+    edge.wait()
+
+    groups_per_tile = LANES // per_group
+    lane_group = lax.broadcasted_iota(jnp.int32, (block, 2 * LANES), 1) % LANES // per_group
+    first = linear == 0
+
+    def tile(t, carry):
+        lanes = pl.ds(pl.multiple_of(t * LANES, LANES), LANES)
+        product = (k_buf[:, lanes].astype(jnp.float32) * v_buf[:, lanes].astype(jnp.float32)).astype(jnp.bfloat16)
+        past = halo[:, lanes]
+        past = jnp.where(first, jnp.zeros_like(past), past)
+        upper, lower = product[:block], product[block:]
+        window = jnp.concatenate(
+            [jnp.concatenate([past, upper], axis=1), jnp.concatenate([upper, lower], axis=1)], axis=0
+        )
+        taps = pattern_ref[pl.ds(pl.multiple_of(t * groups_per_tile, groups_per_tile), groups_per_tile), :]
+        matrices = []
+        for g in range(groups_per_tile):
+            row = jnp.broadcast_to(taps[g : g + 1, :], (block, 2 * block))
+            matrices.append(pltpu.roll(row, 0, 1, stride=1, stride_axis=0).astype(jnp.bfloat16))
+        every = jnp.dot(jnp.concatenate(matrices, axis=0), window, preferred_element_type=jnp.float32)
+        total = every[:block]
+        for g in range(1, groups_per_tile):
+            total = jnp.where(lane_group == g, every[g * block : (g + 1) * block], total)
+        convolved = jnp.concatenate([total[:, :LANES], total[:, LANES:]], axis=0)
+        gated[:, lanes] = (
+            q_buf[:, lanes].astype(jnp.float32)
+            * (convolved + skip_ref[:, lanes] * product.astype(jnp.float32))
+        ).astype(jnp.bfloat16)
+        return carry
+
+    def slot(index, j):
+        return g_full.at[pl.ds(pl.multiple_of(index * rows, rows), rows), j * chunk : (j + 1) * chunk]
+
+    def to_near(j):
+        return remote(gated.at[:, j * chunk : (j + 1) * chunk], slot(me, j), xsend.at[j], xrecv.at[j], near_mate)
+
+    def to_core(j):
+        return remote(gated.at[:, j * chunk : (j + 1) * chunk], slot(me, j), csend.at[j], crecv.at[j], core_mate)
+
+    def pass_on(j):
+        part = slot((1 - near) * 2 + core, j)
+        return remote(part, part, fsend.at[j], frecv.at[j], core_mate)
+
+    tiles = chunk // LANES
+    for j in range(PIECES):
+        lax.fori_loop(j * tiles, (j + 1) * tiles, tile, 0)
+        to_near(j).start()
+        to_core(j).start()
+    mine = pltpu.make_async_copy(gated, g_full.at[pl.ds(pl.multiple_of(me * rows, rows), rows), :], local_sem.at[1])
+    mine.start()
+
+    for p in range(PIECES):
+        to_near(p).wait_recv()
+        pass_on(p).start()
+        for d in range(1, line):
+            along(d, p).wait_recv()
+            across(d, p, group).start()
+    keep.wait()
+    mine.wait()
+    for p in range(PIECES):
+        to_near(p).wait_send()
+        to_core(p).wait()
+        pass_on(p).wait()
+        for d in range(1, line):
+            along(d, p).wait_send()
+            across(d, p, group).wait()
+
+
+def tiled_body(mesh, queries, key_proj, value_proj, filter_taps, skip_gain, out_weight, residual):
+    rows, channels = queries.shape
+    groups_here, block = filter_taps.shape
+    depth, width = out_weight.shape
+    seq_count = mesh.shape["seq"]
+    line = seq_count // 2
+    pattern = jnp.pad(filter_taps.astype(jnp.float32)[:, ::-1], ((0, 0), (1, block - 1)))
+    hbm = pl.BlockSpec(memory_space=pl.ANY)
+    vmem = pl.BlockSpec(memory_space=pltpu.VMEM)
+    dma = pltpu.SemaphoreType.DMA
+    bf16 = jnp.bfloat16
+    g_full, w_full = pl.pallas_call(
+        functools.partial(mixer_kernel, seq_count, channels // groups_here),
+        out_shape=(
+            jax.ShapeDtypeStruct((4 * rows, channels), bf16),
+            jax.ShapeDtypeStruct((depth, line * width), bf16),
+        ),
+        in_specs=[hbm, hbm, hbm, vmem, vmem, hbm],
+        out_specs=(hbm, hbm),
+        scratch_shapes=[pltpu.VMEM((rows, channels), bf16)] * 4
+        + [pltpu.VMEM((block, channels), bf16)] * 2
+        + [dma((3,)), dma((2,)), dma((2,))]
+        + [dma((line - 1, PIECES))] * 4
+        + [dma((PIECES,))] * 6,
+        compiler_params=pltpu.CompilerParams(
+            collective_id=0, has_side_effects=True, vmem_limit_bytes=48 * 2**20
+        ),
+    )(queries, key_proj, value_proj, pattern, skip_gain[None, :], out_weight)
+    out = jnp.dot(g_full, w_full, preferred_element_type=jnp.float32).astype(bf16)
+    seq, core = lax.axis_index("seq"), lax.axis_index("section")
+    me = (seq % 2) * 2 + core
+    pieces = []
+    for m in range(4):
+        part = lax.dynamic_slice_in_dim(out, jnp.bitwise_xor(me, m) * rows, rows, 0)
+        if m:
+            part = lax.ppermute(part, ("seq", "section"), [(i, i ^ m) for i in range(seq_count * 2)])
+        pieces.append(part.reshape(rows, line, width))
+    columns = []
+    for target in range(4):
+        m = jnp.bitwise_xor(me, target)
+        columns.append(jnp.where(m < 2, jnp.where(m == 0, pieces[0], pieces[1]), jnp.where(m == 2, pieces[2], pieces[3])))
+    projected = jnp.stack(columns, axis=2).reshape(rows, line * 4 * width)
+    return (residual.astype(jnp.float32) + projected.astype(jnp.float32)).astype(bf16)
+
+
+def choose(mesh, *args):
+    rows, channels = args[0].shape
+    groups_here, block = args[3].shape
+    if (
+        mesh.shape["chan"] == 1 and mesh.shape["groups"] == 2 and mesh.shape["section"] == 2
+        and mesh.shape["seq"] % 2 == 0 and mesh.shape["seq"] >= 4
+        and block == LANES and rows == 2 * block and channels // groups_here * 8 == LANES
+    ):
+        return tiled_body(mesh, *args)
+    return body(*args)
+
+
 def solution(mesh):
     return jax.shard_map(
-        body,
+        functools.partial(choose, mesh),
         mesh=mesh,
         in_specs=(
             P(("groups", "seq", "section"), "chan"),

time: 432 us -> 317 us (0.73)
  the two profiles are of different devices: /device:TPU:0 before, /device:TPU:11 now
where the time goes in v1:
time: 317 us; the launch traced here: 316 us
  Pallas kernels  243 us (77%)
  matrix products  22.1 us (7%)
  waiting for transfers between devices  20.9 us (7%)
  local copies, waits for them, and re-layouts  17.6 us (6%)
  other arithmetic  8.28 us (3%)
  starting transfers between devices  4.3 us (1%)
    pallas_call x1, Pallas kernels, tiled_body(): pl.pallas_call(functools.partial(mixer_kernel, seq_count, channels // gro...  243 us
    dot_general x1, matrix products, tiled_body(): jnp.dot(g_full, w_full, preferred_element_type=jnp.float32).astype(bf16)  22.1 us
    ppermute x3, waiting for transfers between devices, tiled_body(): lax.ppermute(part, ('seq', 'section'), [(i, i ^ m) for i in range(seq_cou...  20.9 us
    convert_element_type x2, local copies, waits for them, and re-layouts, tiled_body(): projected.astype(jnp.float32)  11.5 us
  transfers between devices with their start and end apart: 3, of which 2 were waited for; matrix products, arithmetic and copies ran while one was open for 0% of the time, Pallas kernels for 0%

profile of v1, /device:TPU:11, one launch (start us, length us, event | category | flops | bytes accessed | tf_op | source)
XLA Modules:
  0.0 316.5 jit_solution(9887020089774269763)
XLA Ops:
  0.0 1.8 rev.3
  1.8 0.2 pad.4.pattern_ref
  2.0 0.0 copy-start
  2.0 2.2 copy-done
  4.2 0.0 copy-start.1
  4.2 0.8 copy-done.1
  4.9 243.3 %shard_map.73 = (bf16[1024,8192]{1,0:T(8,128)(2,1)}, bf16[8192,1024]{1,0:T(8,128)(2,1)}) custom-call(bf16[256,8192]{1,0:T(8,128)(2,1)S(1)} %copy-done, bf16[256,8192]{1,0:T(8,128)(2,1)} %k_hbm.1, bf16[256,8192]{1,0:T(8,128)(2,1)} %v_hbm.1, f32[512,256]{1,0:T(8,128)S(1)} %pad.4.pattern_ref, f32[1,8192]{1,0:T(1,128)S(1)} %bitcast.7, bf16[8192,256]{1,0:T(8,128)(2,1)} %w_hbm.1), custom_call_target="tpu_custom_call" | custom-call | tf_op jit(solution)/shard_map/pallas_call | solution.py:228
  248.2 22.1 %convolution_convert_fusion = bf16[1024,1024]{0,1:T(8,128)(2,1)S(1)} fusion(bf16[1024,8192]{1,0:T(8,128)(2,1)} %get-tuple-element.7, bf16[8192,1024]{1,0:T(8,128)(2,1)} %get-tuple-element.8), kind=kOutput, calls=%fused_computation.2 | convolution fusion | flops 17180917760 | bytes 35651584 | tf_op jit(solution)/shard_map/dot_general | solution.py:245
  270.3 1.2 constant_dynamic-slice_fusion.2
  271.5 0.0 collective-permute-start.1
  271.5 4.3 %collective-permute-start.2 = (bf16[256,1024]{0,1:T(8,128)(2,1)}, bf16[256,1024]{0,1:T(8,128)(2,1)}, u32[]{:S(2)}, u32[]{:S(2)}) collective-permute-start(bf16[256,1024]{0,1:T(8,128)(2,1)} %get-tuple-element.14), channel_id=1, source_target_pairs={{0,3},{1,2},{2,1},{3,0},{4,7},{5,6},{6,5},{7,4},{8,11},{9,10},{10,... | collective-permute-start | bytes 1572872 | tf_op jit(solution)/shard_map/ppermute | solution.py:252
  275.8 0.0 collective-permute-start
  275.8 6.7 %collective-permute-done.1 = bf16[256,1024]{0,1:T(8,128)(2,1)S(1)} collective-permute-done((bf16[256,1024]{0,1:T(8,128)(2,1)}, bf16[256,1024]{0,1:T(8,128)(2,1)S(1)}, u32[]{:S(2)}, u32[]{:S(2)}) %collective-permute-start.1) | collective-permute-done | bytes 524320 | tf_op jit(solution)/shard_map/ppermute | solution.py:252
  282.4 14.2 %collective-permute-done.2 = bf16[256,1024]{0,1:T(8,128)(2,1)} collective-permute-done((bf16[256,1024]{0,1:T(8,128)(2,1)}, bf16[256,1024]{0,1:T(8,128)(2,1)}, u32[]{:S(2)}, u32[]{:S(2)}) %collective-permute-start.2) | collective-permute-done | bytes 524320 | tf_op jit(solution)/shard_map/ppermute | solution.py:252
  296.7 0.0 collective-permute-done
  296.7 1.9 select_select_fusion.3
  298.6 2.3 maximum_convert_fusion
  300.9 5.6 %copy.8 = f32[256,4,4,256]{3,2,1,0:T(4,128)} copy(f32[256,4,4,256]{0,3,1,2:T(8,128)} %maximum_convert_fusion) | data formatting | bytes 8388608 | tf_op jit(solution)/shard_map/convert_element_type | solution.py:259
  306.5 0.0 copy-start.2
  306.5 6.0 %reshape.179 = f32[256,4096]{1,0:T(8,128)} reshape(f32[256,4,4,256]{3,2,1,0:T(4,128)} %copy.8) | data formatting | bytes 8388608 | tf_op jit(solution)/shard_map/convert_element_type | solution.py:259
  312.4 0.0 copy-done.2
  312.4 4.1 %add_convert_fusion = bf16[256,4096]{1,0:T(8,128)(2,1)} fusion(f32[256,4096]{1,0:T(8,128)} %reshape.179, bf16[256,4096]{1,0:T(8,128)(2,1)S(1)} %copy-done.2), kind=kLoop, calls=%fused_computation | loop fusion | flops 3145728 | bytes 8388608 | tf_op jit(solution)/shard_map/convert_element_type | solution.py:259
Async XLA Ops:
  2.0 2.2 copy-start
  4.2 0.8 copy-start.1
  271.5 11.0 %collective-permute-start.1 = (bf16[256,1024]{0,1:T(8,128)(2,1)}, bf16[256,1024]{0,1:T(8,128)(2,1)S(1)}, u32[]{:S(2)}, u32[]{:S(2)}) collective-permute-start(bf16[256,1024]{0,1:T(8,128)(2,1)} %get-tuple-element.15), channel_id=1, source_target_pairs={{0,2},{1,3},{2,0},{3,1},{4,6},{5,7},{6,4},{7,5},{8,10},{9,11},{10,... | collective-permute-start | bytes 1572872 | tf_op jit(solution)/shard_map/ppermute | solution.py:252
  271.5 25.2 %collective-permute-start.2 = (bf16[256,1024]{0,1:T(8,128)(2,1)}, bf16[256,1024]{0,1:T(8,128)(2,1)}, u32[]{:S(2)}, u32[]{:S(2)}) collective-permute-start(bf16[256,1024]{0,1:T(8,128)(2,1)} %get-tuple-element.14), channel_id=1, source_target_pairs={{0,3},{1,2},{2,1},{3,0},{4,7},{5,6},{6,5},{7,4},{8,11},{9,10},{10,... | collective-permute-start | bytes 1572872 | tf_op jit(solution)/shard_map/ppermute | solution.py:252
  275.8 20.9 %collective-permute-start = (bf16[256,1024]{0,1:T(8,128)(2,1)S(1)}, bf16[256,1024]{0,1:T(8,128)(2,1)}, u32[]{:S(2)}, u32[]{:S(2)}) collective-permute-start(bf16[256,1024]{0,1:T(8,128)(2,1)S(1)} %get-tuple-element.13), channel_id=1, source_target_pairs={{0,1},{1,0},{2,3},{3,2},{4,5},{5,4},{6,7},{7,6},{8,9},{9,8},{10,11... | collective-permute-start | bytes 1572872 | tf_op jit(solution)/shard_map/ppermute | solution.py:252
  306.5 6.0 %copy-start.2 = (bf16[256,4096]{1,0:T(8,128)(2,1)S(1)}, bf16[256,4096]{1,0:T(8,128)(2,1)}, u32[]{:S(2)}) copy-start(bf16[256,4096]{1,0:T(8,128)(2,1)} %param.13) | copy-start | bytes 6291460

commit v2 on v1

--- a/solution.py
+++ b/solution.py
@@ -67,10 +67,10 @@
 
 def mixer_kernel(
     seq_count, per_group,
-    q_hbm, k_hbm, v_hbm, pattern_ref, skip_ref, w_hbm,
-    g_full, w_full,
-    q_buf, k_buf, v_buf, gated, tail, halo,
-    load_sem, local_sem, halo_sem, zsend, zrecv, ysend, yrecv, xsend, xrecv, csend, crecv, fsend, frecv,
+    q_hbm, k_hbm, v_hbm, pattern_ref, skip_ref, w_hbm, res_ref,
+    out_ref, w_full,
+    q_buf, k_buf, v_buf, g_buf, tail, halo, total_buf, w_buf, leaving, arriving,
+    load_sem, local_sem, halo_sem, hsend, zsend, zrecv, ysend, yrecv, xsend, xrecv, csend, crecv, fsend, frecv, osend, orecv,
 ):
     group, seq, chan, core = (lax.axis_index(a) for a in ("groups", "seq", "chan", "section"))
     far, near = seq // 2, seq % 2
@@ -130,19 +130,60 @@
     edge = remote(tail, halo, halo_sem.at[0], halo_sem.at[1], after)
     edge.start()
 
-    def along(d, p):
-        return remote(
-            w_hbm.at[span(group, p), :], w_full.at[span(group, p), cols(far)],
-            zsend.at[d - 1, p], zrecv.at[d - 1, p], peers[d - 1],
-        )
+    def source(d):
+        return lax.rem(far + line - d, line)
+
+    def along_z(src, dst, send, d, p, step):
+        return remote(src, dst, send, zrecv.at[d - 1, p], place((far + step) * 2 + near, core))
+
+    def own_right(p):
+        return along_z(w_hbm.at[span(group, p), :], w_full.at[span(group, p), cols(far)], hsend.at[0, p], 1, p, 1)
+
+    def own_left(p):
+        return along_z(w_hbm.at[span(group, p), :], w_full.at[span(group, p), cols(far)], hsend.at[1, p], line - 1, p, -1)
+
+    def onward(d, p, step):
+        part = w_full.at[span(group, p), cols(source(d))]
+        return along_z(part, part, zsend.at[d - 1, p], d + step, p, step)
 
     def across(d, p, which):
-        part = w_full.at[span(which, p), cols(lax.rem(far + line - d, line))]
+        part = w_full.at[span(which, p), cols(source(d))]
         return remote(part, part, ysend.at[d - 1, p], yrecv.at[d - 1, p], group_mate)
 
+    order = [sorted(range(1, line), key=lambda d, z=z: d if d <= z else line - d) for z in range(line)]
+
+    def nth(k):
+        return sum((far == z).astype(jnp.int32) * order[z][k] for z in range(line))
+
+    def goes_right(d):
+        return (far >= d) & (far < line - 1)
+
+    def goes_left(d):
+        return (far < d) & (far > 0)
+
+    def hand_on(k, p):
+        d = nth(k)
+        part = w_full.at[span(group, p), cols(source(d))]
+        remote(part, part, zsend.at[d - 1, p], zrecv.at[d - 1, p], group_mate).wait_recv()
+
+        @pl.when(goes_right(d))
+        def _():
+            onward(d, p, 1).start()
+
+        @pl.when(goes_left(d))
+        def _():
+            onward(d, p, -1).start()
+
+        across(d, p, group).start()
+
     for p in range(PIECES):
-        for d in range(1, line):
-            along(d, p).start()
+        @pl.when(far < line - 1)
+        def _():
+            own_right(p).start()
+
+        @pl.when(far > 0)
+        def _():
+            own_left(p).start()
 
     loads[2].wait()
     edge.wait()
@@ -150,6 +191,8 @@
     groups_per_tile = LANES // per_group
     lane_group = lax.broadcasted_iota(jnp.int32, (block, 2 * LANES), 1) % LANES // per_group
     first = linear == 0
+    my_rows = pl.ds(pl.multiple_of(me * rows, rows), rows)
+    total_buf[...] = jnp.zeros_like(total_buf)
 
     def tile(t, carry):
         lanes = pl.ds(pl.multiple_of(t * LANES, LANES), LANES)
@@ -170,20 +213,20 @@
         for g in range(1, groups_per_tile):
             total = jnp.where(lane_group == g, every[g * block : (g + 1) * block], total)
         convolved = jnp.concatenate([total[:, :LANES], total[:, LANES:]], axis=0)
-        gated[:, lanes] = (
+        g_buf[my_rows, lanes] = (
             q_buf[:, lanes].astype(jnp.float32)
             * (convolved + skip_ref[:, lanes] * product.astype(jnp.float32))
         ).astype(jnp.bfloat16)
         return carry
 
     def slot(index, j):
-        return g_full.at[pl.ds(pl.multiple_of(index * rows, rows), rows), j * chunk : (j + 1) * chunk]
+        return g_buf.at[pl.ds(pl.multiple_of(index * rows, rows), rows), j * chunk : (j + 1) * chunk]
 
     def to_near(j):
-        return remote(gated.at[:, j * chunk : (j + 1) * chunk], slot(me, j), xsend.at[j], xrecv.at[j], near_mate)
+        return remote(slot(me, j), slot(me, j), xsend.at[j], xrecv.at[j], near_mate)
 
     def to_core(j):
-        return remote(gated.at[:, j * chunk : (j + 1) * chunk], slot(me, j), csend.at[j], crecv.at[j], core_mate)
+        return remote(slot(me, j), slot(me, j), csend.at[j], crecv.at[j], core_mate)
 
     def pass_on(j):
         part = slot((1 - near) * 2 + core, j)
@@ -194,24 +237,93 @@
         lax.fori_loop(j * tiles, (j + 1) * tiles, tile, 0)
         to_near(j).start()
         to_core(j).start()
-    mine = pltpu.make_async_copy(gated, g_full.at[pl.ds(pl.multiple_of(me * rows, rows), rows), :], local_sem.at[1])
-    mine.start()
+        if j == PIECES - 2:
+            for p in range(PIECES // 2):
+                hand_on(0, p)
+    for p in range(PIECES // 2, PIECES):
+        hand_on(0, p)
+
+    def relay(j):
+        to_near(j).wait_recv()
+        pass_on(j).start()
 
     for p in range(PIECES):
-        to_near(p).wait_recv()
-        pass_on(p).start()
+        relay(p)
+        for k in range(1, line - 2):
+            hand_on(k, p)
+    keep.wait()
+
+    def multiply(which, p):
+        load = pltpu.make_async_copy(w_full.at[span(which, p), :], w_buf, local_sem.at[1])
+        load.start()
+        load.wait()
+
+        def rows_of(r, carry):
+            at = pl.ds(pl.multiple_of(r * rows, rows), rows)
+            total_buf[at, :] += jnp.dot(g_buf[at, span(which, p)], w_buf[...], preferred_element_type=jnp.float32)
+            return carry
+
+        lax.fori_loop(0, 4, rows_of, 0)
+
+    def from_mate(p):
         for d in range(1, line):
-            along(d, p).wait_recv()
-            across(d, p, group).start()
-    keep.wait()
-    mine.wait()
+            across(d, p, 1 - group).wait_recv()
+        multiply(1 - group, p)
+
+    for p in range(PIECES):
+        hand_on(line - 2, p)
+        if p == 0:
+            for j in range(PIECES):
+                to_core(j).wait_recv()
+                pass_on(j).wait_recv()
+        multiply(group, p)
+        if p:
+            from_mate(p - 1)
+    from_mate(PIECES - 1)
+
+    def other(m):
+        return (1 - near if m >= 2 else near), (1 - core if m % 2 else core)
+
+    def give(m):
+        n, c = other(m)
+        return remote(leaving.at[m - 1], arriving.at[m - 1], osend.at[m - 1], orecv.at[m - 1], place(far * 2 + n, c))
+
+    for m in (3, 2, 1):
+        n, c = other(m)
+        at = pl.ds(pl.multiple_of((n * 2 + c) * rows, rows), rows)
+        leaving[m - 1] = total_buf[at, :].astype(jnp.bfloat16)
+        give(m).start()
+
+    for m in (0, 1, 2, 3):
+        n, c = other(m)
+        if m:
+            give(m).wait()
+        for z in range(line):
+            at = pl.ds(pl.multiple_of((z * 4 + n * 2 + c) * width, width), width)
+            here = slice(z * width, (z + 1) * width)
+            part = arriving[m - 1, :, here].astype(jnp.float32) if m else total_buf[my_rows, here]
+            out_ref[:, at] = (res_ref[:, at].astype(jnp.float32) + part).astype(jnp.bfloat16)
+
     for p in range(PIECES):
         to_near(p).wait_send()
-        to_core(p).wait()
-        pass_on(p).wait()
+        to_core(p).wait_send()
+        pass_on(p).wait_send()
+
+        @pl.when(far < line - 1)
+        def _():
+            own_right(p).wait_send()
+
+        @pl.when(far > 0)
+        def _():
+            own_left(p).wait_send()
+
         for d in range(1, line):
-            along(d, p).wait_send()
-            across(d, p, group).wait()
+            @pl.when(goes_right(d) | goes_left(d))
+            def _():
+                part = w_full.at[span(group, p), cols(source(d))]
+                remote(part, part, zsend.at[d - 1, p], zrecv.at[d - 1, p], group_mate).wait_send()
+
+            across(d, p, group).wait_send()
 
 
 def tiled_body(mesh, queries, key_proj, value_proj, filter_taps, skip_gain, out_weight, residual):
@@ -225,38 +337,28 @@
     vmem = pl.BlockSpec(memory_space=pltpu.VMEM)
     dma = pltpu.SemaphoreType.DMA
     bf16 = jnp.bfloat16
-    g_full, w_full = pl.pallas_call(
+    out, _ = pl.pallas_call(
         functools.partial(mixer_kernel, seq_count, channels // groups_here),
         out_shape=(
-            jax.ShapeDtypeStruct((4 * rows, channels), bf16),
+            jax.ShapeDtypeStruct(residual.shape, bf16),
             jax.ShapeDtypeStruct((depth, line * width), bf16),
         ),
-        in_specs=[hbm, hbm, hbm, vmem, vmem, hbm],
-        out_specs=(hbm, hbm),
-        scratch_shapes=[pltpu.VMEM((rows, channels), bf16)] * 4
+        in_specs=[hbm, hbm, hbm, vmem, vmem, hbm, vmem],
+        out_specs=(vmem, hbm),
+        scratch_shapes=[pltpu.VMEM((rows, channels), bf16)] * 3
+        + [pltpu.VMEM((4 * rows, channels), bf16)]
         + [pltpu.VMEM((block, channels), bf16)] * 2
-        + [dma((3,)), dma((2,)), dma((2,))]
+        + [pltpu.VMEM((4 * rows, line * width), jnp.float32), pltpu.VMEM((depth // (2 * PIECES), line * width), bf16)]
+        + [pltpu.VMEM((3, rows, line * width), bf16)] * 2
+        + [dma((3,)), dma((2,)), dma((2,)), dma((2, PIECES))]
         + [dma((line - 1, PIECES))] * 4
-        + [dma((PIECES,))] * 6,
+        + [dma((PIECES,))] * 6
+        + [dma((3,))] * 2,
         compiler_params=pltpu.CompilerParams(
-            collective_id=0, has_side_effects=True, vmem_limit_bytes=48 * 2**20
+            collective_id=0, has_side_effects=True, vmem_limit_bytes=60 * 2**20
         ),
-    )(queries, key_proj, value_proj, pattern, skip_gain[None, :], out_weight)
-    out = jnp.dot(g_full, w_full, preferred_element_type=jnp.float32).astype(bf16)
-    seq, core = lax.axis_index("seq"), lax.axis_index("section")
-    me = (seq % 2) * 2 + core
-    pieces = []
-    for m in range(4):
-        part = lax.dynamic_slice_in_dim(out, jnp.bitwise_xor(me, m) * rows, rows, 0)
-        if m:
-            part = lax.ppermute(part, ("seq", "section"), [(i, i ^ m) for i in range(seq_count * 2)])
-        pieces.append(part.reshape(rows, line, width))
-    columns = []
-    for target in range(4):
-        m = jnp.bitwise_xor(me, target)
-        columns.append(jnp.where(m < 2, jnp.where(m == 0, pieces[0], pieces[1]), jnp.where(m == 2, pieces[2], pieces[3])))
-    projected = jnp.stack(columns, axis=2).reshape(rows, line * 4 * width)
-    return (residual.astype(jnp.float32) + projected.astype(jnp.float32)).astype(bf16)
+    )(queries, key_proj, value_proj, pattern, skip_gain[None, :], out_weight, residual)
+    return out
 
 
 def choose(mesh, *args):
@@ -264,7 +366,7 @@
     groups_here, block = args[3].shape
     if (
         mesh.shape["chan"] == 1 and mesh.shape["groups"] == 2 and mesh.shape["section"] == 2
-        and mesh.shape["seq"] % 2 == 0 and mesh.shape["seq"] >= 4
+        and mesh.shape["seq"] % 2 == 0 and mesh.shape["seq"] >= 6
         and block == LANES and rows == 2 * block and channels // groups_here * 8 == LANES
     ):
         return tiled_body(mesh, *args)

time: 317 us -> 235 us (0.74)
  the two profiles are of different devices: /device:TPU:11 before, /device:TPU:0 now
where the time goes in v2:
time: 235 us
  Pallas kernels  229 us (97%)
  local copies, waits for them, and re-layouts  5.88 us (3%)
    pallas_call x1, Pallas kernels, tiled_body(): pl.pallas_call(functools.partial(mixer_kernel, seq_count, channels // gro...  229 us

profile of v2, /device:TPU:0, one launch (start us, length us, event | category | flops | bytes accessed | tf_op | source)
XLA Modules:
  0.0 234.5 jit_solution(1733266309536534730)
XLA Ops:
  0.0 1.8 rev.3
  1.8 1.0 pad.4.pattern_ref
  2.8 228.6 %shard_map.73 = (bf16[256,4096]{1,0:T(8,128)(2,1)}, bf16[8192,1024]{1,0:T(8,128)(2,1)}) custom-call(bf16[256,8192]{1,0:T(8,128)(2,1)} %q_hbm.1, bf16[256,8192]{1,0:T(8,128)(2,1)} %k_hbm.1, bf16[256,8192]{1,0:T(8,128)(2,1)} %v_hbm.1, f32[512,256]{1,0:T(8,128)} %pad.4.pattern_ref, f32[1,8192]{1,0:T(1,128)} %bitcast.1, bf16[8192,256]{1,0:T(8,128)(2,1)} %w_hbm.1, ...), custom_call_target="tpu_custom_call" | custom-call | tf_op jit(solution)/shard_map/pallas_call | solution.py:340
  231.4 3.1 %copy.9 = bf16[256,4096]{1,0:T(8,128)(2,1)} copy(bf16[256,4096]{1,0:T(8,128)(2,1)} %get-tuple-element.6) | data formatting | bytes 4194304

commit v3 on v2

--- a/solution.py
+++ b/solution.py
@@ -62,7 +62,7 @@
 
 
 LANES = 128
-PIECES = 4
+PIECES = 8
 
 
 def mixer_kernel(
@@ -128,7 +128,16 @@
         k_buf[rows - block :, :].astype(jnp.float32) * v_buf[rows - block :, :].astype(jnp.float32)
     ).astype(jnp.bfloat16)
     edge = remote(tail, halo, halo_sem.at[0], halo_sem.at[1], after)
-    edge.start()
+    first, last = linear == 0, linear == seq_count * 2 - 1
+
+    @pl.when(jnp.logical_not(last))
+    def _():
+        edge.start()
+
+    @pl.when(first)
+    def _():
+        halo[...] = jnp.zeros_like(halo)
+
 
     def source(d):
         return lax.rem(far + line - d, line)
@@ -186,19 +195,23 @@
             own_left(p).start()
 
     loads[2].wait()
-    edge.wait()
+
+    @pl.when(jnp.logical_not(last))
+    def _():
+        edge.wait_send()
+
+    @pl.when(jnp.logical_not(first))
+    def _():
+        edge.wait_recv()
 
     groups_per_tile = LANES // per_group
     lane_group = lax.broadcasted_iota(jnp.int32, (block, 2 * LANES), 1) % LANES // per_group
-    first = linear == 0
     my_rows = pl.ds(pl.multiple_of(me * rows, rows), rows)
-    total_buf[...] = jnp.zeros_like(total_buf)
 
     def tile(t, carry):
         lanes = pl.ds(pl.multiple_of(t * LANES, LANES), LANES)
         product = (k_buf[:, lanes].astype(jnp.float32) * v_buf[:, lanes].astype(jnp.float32)).astype(jnp.bfloat16)
         past = halo[:, lanes]
-        past = jnp.where(first, jnp.zeros_like(past), past)
         upper, lower = product[:block], product[block:]
         window = jnp.concatenate(
             [jnp.concatenate([past, upper], axis=1), jnp.concatenate([upper, lower], axis=1)], axis=0
@@ -232,76 +245,93 @@
         part = slot((1 - near) * 2 + core, j)
         return remote(part, part, fsend.at[j], frecv.at[j], core_mate)
 
+    inner = (far > 0) & (far < line - 1)
     tiles = chunk // LANES
     for j in range(PIECES):
         lax.fori_loop(j * tiles, (j + 1) * tiles, tile, 0)
         to_near(j).start()
         to_core(j).start()
-        if j == PIECES - 2:
-            for p in range(PIECES // 2):
-                hand_on(0, p)
-    for p in range(PIECES // 2, PIECES):
-        hand_on(0, p)
+        hand_on(0, j)
+
+        @pl.when(inner)
+        def _():
+            hand_on(1, j)
 
     def relay(j):
         to_near(j).wait_recv()
         pass_on(j).start()
 
     for p in range(PIECES):
-        relay(p)
-        for k in range(1, line - 2):
-            hand_on(k, p)
+        @pl.when(inner)
+        def _():
+            hand_on(2, p)
+
+        @pl.when(jnp.logical_not(inner))
+        def _():
+            hand_on(1, p)
+
+        if p % 2:
+            relay(p // 2)
     keep.wait()
 
-    def multiply(which, p):
-        load = pltpu.make_async_copy(w_full.at[span(which, p), :], w_buf, local_sem.at[1])
+    def other(m):
+        return (1 - near if m >= 2 else near), (1 - core if m % 2 else core)
+
+    def give(m, k):
+        n, c = other(m)
+        return remote(
+            leaving.at[m - 1, k], arriving.at[m - 1, k], osend.at[m - 1, k], orecv.at[m - 1, k], place(far * 2 + n, c)
+        )
+
+    def strip(k):
+        return cols(source(nth(k)) if k < line - 1 else far)
+
+    def finish(k):
+        if k < line - 1:
+            for p in range(PIECES):
+                across(nth(k), p, 1 - group).wait_recv()
+        load = pltpu.make_async_copy(w_full.at[:, strip(k)], w_buf, local_sem.at[1])
         load.start()
         load.wait()
 
         def rows_of(r, carry):
             at = pl.ds(pl.multiple_of(r * rows, rows), rows)
-            total_buf[at, :] += jnp.dot(g_buf[at, span(which, p)], w_buf[...], preferred_element_type=jnp.float32)
+            total_buf[at, strip(k)] = jnp.dot(g_buf[at, :], w_buf[...], preferred_element_type=jnp.float32)
             return carry
 
         lax.fori_loop(0, 4, rows_of, 0)
-
-    def from_mate(p):
-        for d in range(1, line):
-            across(d, p, 1 - group).wait_recv()
-        multiply(1 - group, p)
+        for m in (3, 2, 1):
+            n, c = other(m)
+            at = pl.ds(pl.multiple_of((n * 2 + c) * rows, rows), rows)
+            leaving[m - 1, k] = total_buf[at, strip(k)].astype(jnp.bfloat16)
+            give(m, k).start()
 
     for p in range(PIECES):
-        hand_on(line - 2, p)
-        if p == 0:
+        @pl.when(jnp.logical_not(inner))
+        def _():
+            hand_on(2, p)
+
+        if p < PIECES // 2:
+            relay(PIECES // 2 + p)
+        elif p == PIECES // 2:
             for j in range(PIECES):
                 to_core(j).wait_recv()
                 pass_on(j).wait_recv()
-        multiply(group, p)
-        if p:
-            from_mate(p - 1)
-    from_mate(PIECES - 1)
-
-    def other(m):
-        return (1 - near if m >= 2 else near), (1 - core if m % 2 else core)
-
-    def give(m):
-        n, c = other(m)
-        return remote(leaving.at[m - 1], arriving.at[m - 1], osend.at[m - 1], orecv.at[m - 1], place(far * 2 + n, c))
-
-    for m in (3, 2, 1):
-        n, c = other(m)
-        at = pl.ds(pl.multiple_of((n * 2 + c) * rows, rows), rows)
-        leaving[m - 1] = total_buf[at, :].astype(jnp.bfloat16)
-        give(m).start()
-
-    for m in (0, 1, 2, 3):
-        n, c = other(m)
-        if m:
-            give(m).wait()
-        for z in range(line):
+            finish(line - 1)
+        elif p == PIECES // 2 + 1:
+            finish(0)
+        elif p == PIECES // 2 + 2:
+            finish(1)
+    finish(2)
+
+    for k in (3, 0, 1, 2):
+        z = source(nth(k)) if k < line - 1 else far
+        for m in (0, 1, 2, 3):
+            n, c = other(m)
+            if m:
+                give(m, k).wait()
             at = pl.ds(pl.multiple_of((z * 4 + n * 2 + c) * width, width), width)
-            here = slice(z * width, (z + 1) * width)
-            part = arriving[m - 1, :, here].astype(jnp.float32) if m else total_buf[my_rows, here]
+            part = arriving[m - 1, k].astype(jnp.float32) if m else total_buf[my_rows, strip(k)]
             out_ref[:, at] = (res_ref[:, at].astype(jnp.float32) + part).astype(jnp.bfloat16)
 
     for p in range(PIECES):
@@ -348,12 +378,12 @@
         scratch_shapes=[pltpu.VMEM((rows, channels), bf16)] * 3
         + [pltpu.VMEM((4 * rows, channels), bf16)]
         + [pltpu.VMEM((block, channels), bf16)] * 2
-        + [pltpu.VMEM((4 * rows, line * width), jnp.float32), pltpu.VMEM((depth // (2 * PIECES), line * width), bf16)]
-        + [pltpu.VMEM((3, rows, line * width), bf16)] * 2
+        + [pltpu.VMEM((4 * rows, line * width), jnp.float32), pltpu.VMEM((depth, width), bf16)]
+        + [pltpu.VMEM((3, line, rows, width), bf16)] * 2
         + [dma((3,)), dma((2,)), dma((2,)), dma((2, PIECES))]
         + [dma((line - 1, PIECES))] * 4
         + [dma((PIECES,))] * 6
-        + [dma((3,))] * 2,
+        + [dma((3, line))] * 2,
         compiler_params=pltpu.CompilerParams(
             collective_id=0, has_side_effects=True, vmem_limit_bytes=60 * 2**20
         ),
@@ -366,7 +396,7 @@
     groups_here, block = args[3].shape
     if (
         mesh.shape["chan"] == 1 and mesh.shape["groups"] == 2 and mesh.shape["section"] == 2
-        and mesh.shape["seq"] % 2 == 0 and mesh.shape["seq"] >= 6
+        and mesh.shape["seq"] % 2 == 0 and mesh.shape["seq"] == 8
         and block == LANES and rows == 2 * block and channels // groups_here * 8 == LANES
     ):
         return tiled_body(mesh, *args)

time: 235 us -> 210 us (0.89); the launches traced: 235 us -> 206 us
  Pallas kernels: 229 us -> 201 us
    pallas_call x1, Pallas kernels: 229 us -> 201 us  [tiled_body(): pl.pallas_call(functools.partial(mixer_kernel, seq_count, channels // gro...]
where the time goes in v3:
time: 210 us; the launch traced here: 206 us
  Pallas kernels  201 us (96%)
  local copies, waits for them, and re-layouts  5.88 us (3%)
    pallas_call x1, Pallas kernels, tiled_body(): pl.pallas_call(functools.partial(mixer_kernel, seq_count, channels // gro...  201 us

profile of v3, /device:TPU:0, one launch (start us, length us, event | category | flops | bytes accessed | tf_op | source)
XLA Modules:
  0.0 206.5 jit_solution(11281032401883935893)
XLA Ops:
  0.0 1.8 rev.3
  1.8 1.0 pad.4.pattern_ref
  2.8 200.6 %shard_map.73 = (bf16[256,4096]{1,0:T(8,128)(2,1)}, bf16[8192,1024]{1,0:T(8,128)(2,1)}) custom-call(bf16[256,8192]{1,0:T(8,128)(2,1)} %q_hbm.1, bf16[256,8192]{1,0:T(8,128)(2,1)} %k_hbm.1, bf16[256,8192]{1,0:T(8,128)(2,1)} %v_hbm.1, f32[512,256]{1,0:T(8,128)} %pad.4.pattern_ref, f32[1,8192]{1,0:T(1,128)} %bitcast.1, bf16[8192,256]{1,0:T(8,128)(2,1)} %w_hbm.1, ...), custom_call_target="tpu_custom_call" | custom-call | tf_op jit(solution)/shard_map/pallas_call | solution.py:370
  203.3 3.1 %copy.9 = bf16[256,4096]{1,0:T(8,128)(2,1)} copy(bf16[256,4096]{1,0:T(8,128)(2,1)} %get-tuple-element.6) | data formatting | bytes 4194304
